TPU v7x, 32 devices: a whole 2x2x4 slice. The times are simulated.
32 devices in a mesh: gx: 16 (over z, y, core), gy: 2 (over x).
Axes of the slice: x: 2, y: 2, z: 4, core: 2. Of those that a mesh axis runs over, the one named last changes fastest.
Arguments:
- inputs: bfloat16 [128, 8192], P('gy', 'gx'), may hold values from -6 to 6
- gate_pre: bfloat16 [128, 28672], P('gx', 'gy'), may hold values from -8 to 8
- up_pre: bfloat16 [128, 28672], P('gx', 'gy'), may hold values from -6 to 6
- out_grad: bfloat16 [128, 8192], P('gy', 'gx'), may hold values from -6 to 6
- w_gate: bfloat16 [8192, 28672], P('gx', 'gy'), may hold values from -0.0625 to 0.0625
- w_up: bfloat16 [8192, 28672], P('gx', 'gy'), may hold values from -0.0625 to 0.0625
- w_down: bfloat16 [28672, 8192], P('gy', 'gx'), may hold values from -0.03125 to 0.03125
Outputs:
- grad_input: bfloat16 [128, 8192], P('gy', 'gx')
- grad_w_gate: bfloat16 [8192, 28672], P('gx', 'gy')
- grad_w_up: bfloat16 [8192, 28672], P('gx', 'gy')
- grad_w_down: bfloat16 [28672, 8192], P('gy', 'gx')
All inputs are finite; a program needn't handle non-finite values.
Results may differ from a plain program's by a relative error of at most 0.017.
Values may be sent and summed in bfloat16 or wider, within the bound.
A program may use at most 256 MiB of HBM per device.

v0:
```python
import jax
import jax.numpy as jnp
from jax import lax
from jax.sharding import PartitionSpec as P


def swiglu_back(d_hidden, gate_pre, up_pre):
    gate_val = gate_pre.astype(jnp.float32)
    up_val = up_pre.astype(jnp.float32)
    sig = jax.nn.sigmoid(gate_val)
    silu_val = gate_val * sig
    hidden = (silu_val * up_val).astype(jnp.bfloat16)
    d_up = (d_hidden * silu_val).astype(jnp.bfloat16)
    d_gate = (d_hidden * up_val * sig * (1.0 + gate_val * (1.0 - sig))).astype(jnp.bfloat16)
    return (d_gate, d_up, hidden)


def contract_rows(left, right):
    return lax.dot_general(
        left, right, (((0,), (0,)), ((), ())), preferred_element_type=jnp.float32
    )


def contract_cols(left, right):
    return lax.dot_general(
        left, right, (((1,), (1,)), ((), ())), preferred_element_type=jnp.float32
    )


def per_device(inputs, gate_pre, up_pre, out_grad, w_gate, w_up, w_down):
    input_rows, grad_rows = (
        lax.all_gather(inputs, "gy", axis=0, tiled=True),
        lax.all_gather(out_grad, "gy", axis=0, tiled=True),
    )
    d_hidden = lax.psum_scatter(
        contract_cols(grad_rows, w_down).astype(jnp.bfloat16), "gx", scatter_dimension=0, tiled=True
    ).astype(jnp.float32)
    d_gate, d_up, hidden = swiglu_back(d_hidden, gate_pre, up_pre)
    gate_piece = lax.all_gather(d_gate, "gx", axis=0, tiled=True)
    up_piece = lax.all_gather(d_up, "gx", axis=0, tiled=True)
    hidden_piece = lax.all_gather(hidden, "gx", axis=0, tiled=True)
    gate_total = contract_rows(input_rows, gate_piece)
    up_total = contract_rows(input_rows, up_piece)
    down_total = contract_rows(hidden_piece, grad_rows)
    input_block_grad = contract_cols(gate_piece, w_gate) + contract_cols(up_piece, w_up)
    input_total = input_block_grad
    gate_total, up_total, down_total, input_total = (gate_total, up_total, down_total, input_total)
    grad_input = lax.psum_scatter(
        input_total.astype(jnp.bfloat16), "gy", scatter_dimension=0, tiled=True
    )
    return (
        grad_input,
        gate_total.astype(jnp.bfloat16),
        up_total.astype(jnp.bfloat16),
        down_total.astype(jnp.bfloat16),
    )


def solution(mesh):
    placed = (
        P("gy", "gx"),
        P("gx", "gy"),
        P("gx", "gy"),
        P("gy", "gx"),
        P("gx", "gy"),
        P("gx", "gy"),
        P("gy", "gx"),
    )
    return jax.shard_map(
        per_device,
        mesh=mesh,
        in_specs=placed,
        out_specs=(P("gy", "gx"), P("gx", "gy"), P("gx", "gy"), P("gy", "gx")),
        check_vma=False,
    )
```

profile of v0, /device:TPU:0, one launch (start us, length us, event | category | flops | bytes accessed | tf_op | source)
XLA Modules:
  0.0 300.6 jit_solution(5242010842057136992)
XLA Ops:
  7.2 0.0 copy-start.2
  7.2 0.0 copy-start.1
  7.2 0.0 copy-start.3
  7.2 0.0 reduce-scatter.3.cloned.1.call-start
  7.2 6.2 %all_gather.15 = bf16[128,512]{1,0:T(8,128)(2,1)S(1)} all-gather(bf16[64,512]{1,0:T(8,128)(2,1)} %param.10), channel_id=1, replica_groups=mesh['gx'=16,'gy'=2] {'gy'}, dimensions={0}, use_global_device_ids=true | all-gather | bytes 196608 | tf_op jit(solution)/shard_map/all_gather | solution.py:33
  13.5 11.8 %convolution_convert_fusion.3 = bf16[128,14336]{1,0:T(8,128)(2,1)} fusion(bf16[128,512]{1,0:T(8,128)(2,1)S(1)} %all_gather.15, bf16[14336,512]{1,0:T(8,128)(2,1)} %param.13), kind=kOutput, calls=%fused_computation.5 | convolution fusion | flops 1880883200 | bytes 18481152 | tf_op jit(solution)/shard_map/dot_general | solution.py:25
  25.3 0.0 reduce-scatter.3.cloned.1.call-update
  25.3 0.0 all-gather.4.cloned.1.call-start
  25.4 70.5 %reduce-scatter.3.cloned.1.call-done = bf16[8,14336]{1,0:T(8,128)(2,1)} async-done(((bf16[128,14336]{1,0:T(8,128)(2,1)}), bf16[8,14336]{1,0:T(8,128)(2,1)}) %reduce-scatter.3.cloned.1.call-update) | async-done | bytes 229392 | tf_op jit(solution)/shard_map/reduce_scatter | solution.py:35
  95.9 0.0 copy-done.2
  95.9 0.0 copy-done.1
  95.9 2.0 fusion.7
  97.9 0.0 all-gather.4.cloned.1.call-update
  97.9 0.0 all-gather.6.cloned.1.call-start
  98.0 0.7 all-gather.6.cloned.1.call-update
  98.7 0.0 all-gather.8.cloned.1.call-start
  98.7 0.5 all-gather.8.cloned.1.call-update
  99.2 0.0 reduce-scatter.5.cloned.1.call-start
  99.3 0.0 copy-done.3
  99.3 4.9 %all_gather.18 = bf16[128,512]{1,0:T(8,128)(2,1)S(1)} all-gather(bf16[64,512]{1,0:T(8,128)(2,1)S(1)} %copy-done.3), channel_id=1, replica_groups=mesh['gx'=16,'gy'=2] {'gy'}, dimensions={0}, use_global_device_ids=true | all-gather | bytes 196608 | tf_op jit(solution)/shard_map/all_gather | solution.py:32
  104.2 41.1 %all-gather.4.cloned.1.call-done = bf16[128,14336]{1,0:T(8,128)(2,1)} async-done(((bf16[8,14336]{1,0:T(8,128)(2,1)}), bf16[128,14336]{1,0:T(8,128)(2,1)}) %all-gather.4.cloned.1.call-update) | async-done | bytes 3670032 | tf_op jit(solution)/shard_map/all_gather | solution.py:39
  145.4 11.3 %fusion.12 = f32[128,512]{1,0:T(8,128)S(1)} fusion(bf16[128,14336]{1,0:T(8,128)(2,1)} %all-gather.4.cloned.1.call-done, bf16[512,14336]{1,0:T(8,128)(2,1)} %param.11), kind=kOutput, calls=%fused_computation.23 | convolution fusion | flops 1879048192 | bytes 18612224 | tf_op jit(solution)/shard_map/dot_general | solution.py:25
  156.7 38.4 %all-gather.6.cloned.1.call-done = bf16[128,14336]{1,0:T(8,128)(2,1)} async-done(((bf16[8,14336]{1,0:T(8,128)(2,1)}), bf16[128,14336]{1,0:T(8,128)(2,1)}) %all-gather.6.cloned.1.call-update) | async-done | bytes 3670032 | tf_op jit(solution)/shard_map/all_gather | solution.py:40
  195.1 11.9 %fusion.2 = bf16[128,512]{1,0:T(8,128)(2,1)} fusion(f32[128,512]{1,0:T(8,128)S(1)} %fusion.12, bf16[128,14336]{1,0:T(8,128)(2,1)} %all-gather.6.cloned.1.call-done, bf16[512,14336]{1,0:T(8,128)(2,1)} %param.12), kind=kOutput, calls=%fused_computation.7 | convolution fusion | flops 1879179264 | bytes 18743296 | tf_op jit(solution)/shard_map/dot_general | solution.py:25
  207.1 0.0 reduce-scatter.5.cloned.1.call-update
  207.1 0.0 copy-start
  207.1 10.0 %fusion = bf16[512,14336]{0,1:T(8,128)(2,1)} fusion(bf16[128,14336]{1,0:T(8,128)(2,1)} %all-gather.4.cloned.1.call-done, bf16[128,512]{1,0:T(8,128)(2,1)S(1)} %all_gather.18), kind=kOutput, calls=%fused_computation.3 | convolution fusion | flops 1886388224 | bytes 18481152 | tf_op jit(solution)/shard_map/dot_general | solution.py:19
  217.0 7.5 %fusion.1 = bf16[512,14336]{0,1:T(8,128)(2,1)} fusion(bf16[128,14336]{1,0:T(8,128)(2,1)S(1)} %copy-done, bf16[128,512]{1,0:T(8,128)(2,1)S(1)} %all_gather.18), kind=kOutput, calls=%fused_computation.4 | convolution fusion | flops 1886388224 | bytes 18481152 | tf_op jit(solution)/shard_map/dot_general | solution.py:19
  224.6 20.1 %all-gather.8.cloned.1.call-done = bf16[128,14336]{1,0:T(8,128)(2,1)} async-done(((bf16[8,14336]{1,0:T(8,128)(2,1)}), bf16[128,14336]{1,0:T(8,128)(2,1)}) %all-gather.8.cloned.1.call-update) | async-done | bytes 3670032 | tf_op jit(solution)/shard_map/all_gather | solution.py:41
  244.7 9.6 %convolution_convert_fusion = bf16[14336,512]{1,0:T(8,128)(2,1)} fusion(bf16[128,14336]{1,0:T(8,128)(2,1)} %all-gather.8.cloned.1.call-done, bf16[128,512]{1,0:T(8,128)(2,1)S(1)} %all_gather.15), kind=kOutput, calls=%fused_computation | convolution fusion | flops 1886388224 | bytes 18481152 | tf_op jit(solution)/shard_map/dot_general | solution.py:19
  254.3 19.9 %copy.11 = bf16[512,14336]{1,0:T(8,128)(2,1)} copy(bf16[512,14336]{0,1:T(8,128)(2,1)} %fusion) | data formatting | bytes 29360128
  274.2 19.9 %copy.12 = bf16[512,14336]{1,0:T(8,128)(2,1)} copy(bf16[512,14336]{0,1:T(8,128)(2,1)} %fusion.1) | data formatting | bytes 29360128
  (2 shorter events, 0.0 us)
Async XLA Ops:
  7.2 88.7 %copy-start.2 = (bf16[8,14336]{1,0:T(8,128)(2,1)S(1)}, bf16[8,14336]{1,0:T(8,128)(2,1)}, u32[]{:S(2)}) copy-start(bf16[8,14336]{1,0:T(8,128)(2,1)} %param.8) | copy-start | bytes 688132
  7.2 88.7 %copy-start.1 = (bf16[8,14336]{1,0:T(8,128)(2,1)S(1)}, bf16[8,14336]{1,0:T(8,128)(2,1)}, u32[]{:S(2)}) copy-start(bf16[8,14336]{1,0:T(8,128)(2,1)} %param.9) | copy-start | bytes 688132
  7.2 92.1 %copy-start.3 = (bf16[64,512]{1,0:T(8,128)(2,1)S(1)}, bf16[64,512]{1,0:T(8,128)(2,1)}, u32[]{:S(2)}) copy-start(bf16[64,512]{1,0:T(8,128)(2,1)} %param.7) | copy-start | bytes 196612
  7.2 88.7 %reduce-scatter.3.cloned.1.call-start = ((), (), s32[]{:S(2)}) async-start(), calls=%async_computation.2 | async-start | bytes 3899392 | tf_op jit(solution)/shard_map/reduce_scatter | solution.py:35
  25.3 120.0 %all-gather.4.cloned.1.call-start = ((), (), s32[]{:S(2)}) async-start(), calls=%async_computation.3 | async-start | bytes 3899392 | tf_op jit(solution)/shard_map/all_gather | solution.py:39
  97.9 97.2 %all-gather.6.cloned.1.call-start = ((), (), s32[]{:S(2)}) async-start(), calls=%async_computation.4 | async-start | bytes 3899392 | tf_op jit(solution)/shard_map/all_gather | solution.py:40
  98.7 146.0 %all-gather.8.cloned.1.call-start = ((), (), s32[]{:S(2)}) async-start(), calls=%async_computation.6 | async-start | bytes 3899392 | tf_op jit(solution)/shard_map/all_gather | solution.py:41
  99.2 194.9 %reduce-scatter.5.cloned.1.call-start = ((), (), s32[]{:S(2)}) async-start(), calls=%async_computation.5 | async-start | bytes 196608 | tf_op jit(solution)/shard_map/reduce_scatter | solution.py:48
  207.1 10.0 %copy-start = (bf16[128,14336]{1,0:T(8,128)(2,1)S(1)}, bf16[128,14336]{1,0:T(8,128)(2,1)}, u32[]{:S(2)}) copy-start(bf16[128,14336]{1,0:T(8,128)(2,1)} %all-gather.6.cloned.1.call-done) | copy-start | bytes 11010052
Sparse Core Ops, SparseCore 0:
  25.5 70.3 reduce-scatter.2
  99.0 46.3 all-gather.3
  148.5 46.5 all-gather.5
  198.1 46.5 all-gather.7
  247.4 9.2 reduce-scatter.4
where the time goes:
time: 302 us; the launch traced here: 301 us
  waiting for transfers between devices  171 us (57%)
  matrix products  62.2 us (21%)
  local copies, waits for them, and re-layouts  39.8 us (13%)
  between operations  13.8 us (5%)
  blocking collectives  11.2 us (4%)
    reduce_scatter x1, waiting for transfers between devices, per_device(): lax.psum_scatter(contract_cols(grad_rows, w_down).astype(jnp.bfloat16), '...  70.5 us
    all_gather x1, waiting for transfers between devices, per_device(): gate_piece = lax.all_gather(d_gate, 'gx', axis=0, tiled=True)  41.1 us
    unnamed x10, local copies, waits for them, and re-layouts  39.8 us
    all_gather x1, waiting for transfers between devices, per_device(): up_piece = lax.all_gather(d_up, 'gx', axis=0, tiled=True)  38.4 us
    dot_general x3, matrix products, contract_cols(): lax.dot_general(left, right, (((1,), (1,)), ((), ())), preferred_element_...  35.1 us
    dot_general x3, matrix products, contract_rows(): lax.dot_general(left, right, (((0,), (0,)), ((), ())), preferred_element_...  27.1 us
    all_gather x1, waiting for transfers between devices, per_device(): hidden_piece = lax.all_gather(hidden, 'gx', axis=0, tiled=True)  20.1 us
    all_gather x1, blocking collectives, per_device(): lax.all_gather(out_grad, 'gy', axis=0, tiled=True)  6.24 us
  transfers between devices with their start and end apart: 5, of which 4 were waited for; matrix products, arithmetic and copies ran while one was open for 30% of the time, Pallas kernels for 0%

commit v1 on v0

v1 whole, which is shorter than its diff:
```python
import functools

import jax
import jax.numpy as jnp
from jax import lax
from jax.experimental import pallas as pl
from jax.experimental.pallas import tpu as pltpu
from jax.sharding import PartitionSpec as P

MESH = pl.DeviceIdType.MESH
F32 = jnp.float32
BF16 = jnp.bfloat16
CHUNKS = 7
OUTER = 4


def exchange_kernel(
    sizes,
    x_ref, og_ref, gate_ref, up_ref, wd_ref,
    dh_ref, gates_ref, ups_ref, xs_ref, ogs_ref,
    w_buf, og_buf, part, core_in, sum_core, inner_in, sum_inner, outer_in, own,
    w_sem, local_sem, gy_send, gy_recv,
    rc_send, rc_recv, ri_send, ri_recv, ro_send, ro_recv,
    go_send, go_recv, gi_send, gi_recv, gc_send, gc_recv,
    ho_send, ho_recv, hi_send, hi_recv, hc_send, hc_recv,
    own_sem,
):
    A, B, G, K = sizes
    me = lax.axis_index("gx")
    gy = lax.axis_index("gy")
    core = lax.rem(me, 2)
    b = lax.rem(me // 2, B)
    a = me // (2 * B)
    cw = w_buf.shape[1]
    t = og_ref.shape[0]

    def index(ai, bi, ci):
        return (ai * B + bi) * 2 + ci

    def outer_peer(d):
        return lax.rem(a + d, A)

    def outer_source(d):
        return lax.rem(a + A - d, A)

    def inner_peer(d):
        return lax.rem(b + d, B)

    def inner_source(d):
        return lax.rem(b + B - d, B)

    def remote(src, dst, send, recv, gx_to, gy_to=None):
        return pltpu.make_async_remote_copy(
            src_ref=src, dst_ref=dst, send_sem=send, recv_sem=recv,
            device_id=(gx_to, gy if gy_to is None else gy_to), device_id_type=MESH,
        )

    sibling = index(a, b, 1 - core)

    barrier = pltpu.get_barrier_semaphore()
    pl.semaphore_signal(barrier, inc=1, device_id=(sibling, gy), device_id_type=MESH)
    for d in range(1, A):
        pl.semaphore_signal(barrier, inc=1, device_id=(index(outer_peer(d), b, core), gy), device_id_type=MESH)
    for d in range(1, B):
        pl.semaphore_signal(barrier, inc=1, device_id=(index(a, inner_peer(d), core), gy), device_id_type=MESH)
    for d in range(1, G):
        pl.semaphore_signal(barrier, inc=1, device_id=(me, lax.rem(gy + d, G)), device_id_type=MESH)
    pl.semaphore_wait(barrier, 1 + (A - 1) + (B - 1) + (G - 1))

    def w_copy(k, slot):
        return pltpu.make_async_copy(wd_ref.at[pl.ds(pl.multiple_of(k * cw, cw), cw)], w_buf.at[slot], w_sem.at[slot])

    w_copy(0, 0).start()
    w_copy(1, 1).start()

    def gy_copies(d):
        to = lax.rem(gy + d, G)
        return (
            remote(og_ref, og_buf.at[gy], gy_send.at[0, d - 1], gy_recv.at[0, d - 1], me, to),
            remote(x_ref, xs_ref.at[gy], gy_send.at[1, d - 1], gy_recv.at[1, d - 1], me, to),
        )

    locals_ = [
        pltpu.make_async_copy(og_ref, og_buf.at[gy], local_sem.at[0]),
        pltpu.make_async_copy(x_ref, xs_ref.at[gy], local_sem.at[1]),
        pltpu.make_async_copy(gate_ref, gates_ref.at[me], local_sem.at[2]),
        pltpu.make_async_copy(up_ref, ups_ref.at[me], local_sem.at[3]),
    ]
    locals_[0].start()
    for d in range(1, G):
        gy_copies(d)[0].start()

    def gather_ops(full, outer_s, outer_r, inner_s, inner_r, core_s, core_r):
        def to_outer(src, d):
            return remote(src, full(me), outer_s(d - 1), outer_r(d - 1), index(outer_peer(d), b, core))

        def to_inner(src, ai, d):
            s = index(ai, b, core)
            return remote(src, full(s), inner_s(d - 1, ai), inner_r(d - 1, ai), index(a, inner_peer(d), core))

        def to_core(src, ai, bi):
            s = index(ai, bi, core)
            return remote(src, full(s), core_s(ai * B + bi), core_r(ai * B + bi), sibling)

        return to_outer, to_inner, to_core

    def send_own(ops, src):
        to_outer, to_inner, to_core = ops
        for d in range(1, A):
            to_outer(src, d).start()
        for d in range(1, B):
            to_inner(src, a, d).start()
        to_core(src, a, b).start()

    def pass_outer(ops, full):
        to_outer, to_inner, to_core = ops
        for d in range(1, A):
            to_outer(full(me), d).wait_recv()
            ai = outer_source(d)
            src = full(index(ai, b, core))
            for e in range(1, B):
                to_inner(src, ai, e).start()
            to_core(src, ai, b).start()

    def pass_inner(ops, full):
        to_outer, to_inner, to_core = ops
        for e in range(1, B):
            bi = inner_source(e)
            for d in range(A):
                ai = outer_source(d)
                to_inner(full(me), ai, e).wait_recv()
                to_core(full(index(ai, bi, core)), ai, bi).start()

    def finish(ops, full):
        to_outer, to_inner, to_core = ops
        for d in range(1, A):
            to_outer(full(me), d).wait_send()
        for e in range(1, B):
            for ai in range(A):
                to_inner(full(me), ai, e).wait_send()
        for ai in range(A):
            for bi in range(B):
                to_core(full(me), ai, bi).wait()

    saved = []
    for g, out in enumerate((gates_ref, ups_ref)):
        full = functools.partial(lambda out, s: out.at[s], out)
        ops = gather_ops(
            full,
            functools.partial(lambda g, i: go_send.at[g, i], g),
            functools.partial(lambda g, i: go_recv.at[g, i], g),
            functools.partial(lambda g, i, j: gi_send.at[g, i, j], g),
            functools.partial(lambda g, i, j: gi_recv.at[g, i, j], g),
            functools.partial(lambda g, i: gc_send.at[g, i], g),
            functools.partial(lambda g, i: gc_recv.at[g, i], g),
        )
        saved.append((ops, full))

    send_own(saved[0][0], gate_ref)
    send_own(saved[1][0], up_ref)
    for d in range(1, G):
        gy_copies(d)[1].start()
    for copy in locals_[1:]:
        copy.start()
    locals_[0].wait()
    for d in range(1, G):
        gy_copies(d)[0].wait_recv()
    og_out = pltpu.make_async_copy(og_buf, ogs_ref, local_sem.at[4])
    og_out.start()

    def core_copy(k):
        return remote(part.at[k, :, :, 1 - core], core_in.at[k], rc_send.at[k], rc_recv.at[k], sibling)

    def inner_copy(k, e):
        return remote(
            sum_core.at[k, inner_peer(e)], inner_in.at[k, e - 1],
            ri_send.at[k, e - 1], ri_recv.at[k, e - 1], index(a, inner_peer(e), core),
        )

    def outer_copy(k, d):
        return remote(
            sum_inner.at[k, outer_peer(d)], outer_in.at[k, d - 1],
            ro_send.at[k, d - 1], ro_recv.at[k, d - 1], index(outer_peer(d), b, core),
        )

    def multiply(k, _):
        slot = lax.rem(k, 2)
        w_copy(k, slot).wait()
        og = og_buf[...].reshape(G * t, og_buf.shape[2])
        prod = lax.dot_general(og, w_buf[slot], (((1,), (1,)), ((), ())), preferred_element_type=F32)
        part[k] = prod.reshape(part.shape[1:]).astype(BF16)
        core_copy(k).start()

        @pl.when(k + 2 < K)
        def _():
            w_copy(k + 2, slot).start()
        return 0

    lax.fori_loop(0, K, multiply, 0)

    def add_core(k, _):
        core_copy(k).wait_recv()
        for bi in range(B):
            sum_core[k, bi] = (part[k, :, bi, core].astype(F32) + core_in[k, :, bi].astype(F32)).astype(BF16)
        for e in range(1, B):
            inner_copy(k, e).start()
        return 0

    lax.fori_loop(0, K, add_core, 0)
    for ops, full in saved:
        pass_outer(ops, full)

    def add_inner(k, _):
        total = sum_core[k, b].astype(F32)
        for e in range(1, B):
            inner_copy(k, e).wait_recv()
            total += inner_in[k, e - 1].astype(F32)
        sum_inner[k] = total.astype(BF16)
        for d in range(1, A):
            outer_copy(k, d).start()
        return 0

    lax.fori_loop(0, K, add_inner, 0)
    for ops, full in saved:
        pass_inner(ops, full)

    def hidden_ops(k):
        full = lambda s: dh_ref.at[k, s]
        return gather_ops(
            full,
            lambda i: ho_send.at[k, i], lambda i: ho_recv.at[k, i],
            lambda i, j: hi_send.at[k, i, j], lambda i, j: hi_recv.at[k, i, j],
            lambda i: hc_send.at[k, i], lambda i: hc_recv.at[k, i],
        ), full

    def own_copy(k):
        return pltpu.make_async_copy(own.at[k], dh_ref.at[k, me], own_sem.at[k])

    def add_outer(k, _):
        total = sum_inner[k, a].astype(F32)
        for d in range(1, A):
            outer_copy(k, d).wait_recv()
            total += outer_in[k, d - 1].astype(F32)
        own[k] = total.astype(BF16)
        send_own(hidden_ops(k)[0], own.at[k])
        own_copy(k).start()
        return 0

    lax.fori_loop(0, K, add_outer, 0)

    def forward_outer(k, _):
        pass_outer(*hidden_ops(k))
        return 0

    lax.fori_loop(0, K, forward_outer, 0)

    def forward_inner(k, _):
        pass_inner(*hidden_ops(k))
        return 0

    lax.fori_loop(0, K, forward_inner, 0)

    def close(k, _):
        finish(*hidden_ops(k))
        own_copy(k).wait()
        core_copy(k).wait_send()
        for e in range(1, B):
            inner_copy(k, e).wait_send()
        for d in range(1, A):
            outer_copy(k, d).wait_send()
        return 0

    lax.fori_loop(0, K, close, 0)
    for ops, full in saved:
        finish(ops, full)
    for copy in locals_[1:]:
        copy.wait()
    og_out.wait()
    for d in range(1, G):
        og_copy, x_copy = gy_copies(d)
        og_copy.wait_send()
        x_copy.wait()


def exchange(n, G, x, og, gate, up, wd):
    A = OUTER if n % (2 * OUTER) == 0 else 1
    B = n // (2 * A)
    K = CHUNKS
    t, dl = og.shape
    rows, ffl = gate.shape
    cw = ffl // K
    any_spec = pl.BlockSpec(memory_space=pl.ANY)
    dma = pltpu.SemaphoreType.DMA
    return pl.pallas_call(
        functools.partial(exchange_kernel, (A, B, G, K)),
        out_shape=(
            jax.ShapeDtypeStruct((K, n, rows, cw), BF16),
            jax.ShapeDtypeStruct((n, rows, ffl), BF16),
            jax.ShapeDtypeStruct((n, rows, ffl), BF16),
            jax.ShapeDtypeStruct((G, t, dl), BF16),
            jax.ShapeDtypeStruct((G, t, dl), BF16),
        ),
        in_specs=[any_spec] * 5,
        out_specs=(any_spec,) * 5,
        scratch_shapes=[
            pltpu.VMEM((2, cw, dl), BF16),
            pltpu.VMEM((G, t, dl), BF16),
            pltpu.VMEM((K, A, B, 2, rows, cw), BF16),
            pltpu.VMEM((K, A, B, rows, cw), BF16),
            pltpu.VMEM((K, B, A, rows, cw), BF16),
            pltpu.VMEM((K, max(B - 1, 1), A, rows, cw), BF16),
            pltpu.VMEM((K, A, rows, cw), BF16),
            pltpu.VMEM((K, max(A - 1, 1), rows, cw), BF16),
            pltpu.VMEM((K, rows, cw), BF16),
            dma((2,)), dma((5,)), dma((2, max(G - 1, 1))), dma((2, max(G - 1, 1))),
            dma((K,)), dma((K,)), dma((K, max(B - 1, 1))), dma((K, max(B - 1, 1))),
            dma((K, max(A - 1, 1))), dma((K, max(A - 1, 1))),
            dma((2, max(A - 1, 1))), dma((2, max(A - 1, 1))),
            dma((2, max(B - 1, 1), A)), dma((2, max(B - 1, 1), A)),
            dma((2, A * B)), dma((2, A * B)),
            dma((K, max(A - 1, 1))), dma((K, max(A - 1, 1))),
            dma((K, max(B - 1, 1), A)), dma((K, max(B - 1, 1), A)),
            dma((K, A * B)), dma((K, A * B)),
            dma((K,)),
        ],
        compiler_params=pltpu.CompilerParams(
            collective_id=0, has_side_effects=True, vmem_limit_bytes=32 * 2**20
        ),
    )(x, og, gate, up, wd)


def gate_up_kernel(x_ref, dh_ref, gate_ref, up_ref, wg_ref, wu_ref, gin_ref, gwg_ref, gwu_ref, xt, acc):
    step = pl.program_id(0)
    tokens, dl = x_ref.shape

    @pl.when(step == 0)
    def _():
        xt[...] = x_ref[...].astype(F32).T.astype(BF16)
        acc[...] = jnp.zeros_like(acc)

    width = gate_ref.shape[2]
    g = gate_ref[...].astype(F32).reshape(tokens, width)
    u = up_ref[...].astype(F32).reshape(tokens, width)
    dh = dh_ref[0].astype(F32).reshape(tokens, width)
    s = jax.nn.sigmoid(g)
    d_up = (dh * (g * s)).astype(BF16)
    d_gate = (dh * u * s * (1.0 + g * (1.0 - s))).astype(BF16)
    gwg_ref[...] = jnp.dot(xt[...], d_gate, preferred_element_type=F32).astype(BF16)
    gwu_ref[...] = jnp.dot(xt[...], d_up, preferred_element_type=F32).astype(BF16)
    dims = (((1,), (1,)), ((), ()))
    acc[...] += lax.dot_general(d_gate, wg_ref[...], dims, preferred_element_type=F32) + lax.dot_general(
        d_up, wu_ref[...], dims, preferred_element_type=F32
    )

    @pl.when(step == pl.num_programs(0) - 1)
    def _():
        gin_ref[...] = acc[...].astype(BF16)


def down_kernel(og_ref, gate_ref, up_ref, after_ref, gwd_ref):
    tokens, dl = og_ref.shape
    width = gate_ref.shape[2]
    g = gate_ref[...].astype(F32).reshape(tokens, width)
    u = up_ref[...].astype(F32).reshape(tokens, width)
    hidden = (g * jax.nn.sigmoid(g) * u).astype(BF16)
    gwd_ref[...] = lax.dot_general(
        hidden, og_ref[...], (((0,), (0,)), ((), ())), preferred_element_type=F32
    ).astype(BF16)


def per_device(n, G, inputs, gate_pre, up_pre, out_grad, w_gate, w_up, w_down):
    dh, gates, ups, xs, ogs = exchange(n, G, inputs, out_grad, gate_pre, up_pre, w_down)
    K, _, rows, cw = dh.shape
    dl, ffl = w_gate.shape
    tokens = n * rows
    x = xs.reshape(tokens, dl)
    og = ogs.reshape(tokens, dl)
    width = 1024 if cw % 1024 == 0 else cw
    per = cw // width
    steps = ffl // width
    whole = pl.BlockSpec((tokens, dl), lambda k: (0, 0))
    act = pl.BlockSpec((n, rows, width), lambda k: (0, 0, k))
    wide = pl.BlockSpec((dl, width), lambda k: (0, k))
    gin, gwg, gwu = pl.pallas_call(
        gate_up_kernel,
        grid=(steps,),
        out_shape=(
            jax.ShapeDtypeStruct((tokens, dl), BF16),
            jax.ShapeDtypeStruct((dl, ffl), BF16),
            jax.ShapeDtypeStruct((dl, ffl), BF16),
        ),
        in_specs=[whole, pl.BlockSpec((1, n, rows, width), lambda k: (k // per, 0, 0, k % per)), act, act, wide, wide],
        out_specs=(whole, wide, wide),
        scratch_shapes=[pltpu.VMEM((dl, tokens), BF16), pltpu.VMEM((tokens, dl), F32)],
        compiler_params=pltpu.CompilerParams(vmem_limit_bytes=48 * 2**20),
        cost_estimate=pl.CostEstimate(flops=8 * tokens * dl * ffl, bytes_accessed=8 * dl * ffl, transcendentals=0),
    )(x, dh, gates, ups, w_gate, w_up)
    grad_input = lax.psum_scatter(gin, "gy", scatter_dimension=0, tiled=True)
    gwd = pl.pallas_call(
        down_kernel,
        grid=(steps,),
        out_shape=jax.ShapeDtypeStruct((ffl, dl), BF16),
        in_specs=[whole, act, act, pl.BlockSpec(memory_space=pl.ANY)],
        out_specs=pl.BlockSpec((width, dl), lambda k: (k, 0)),
        compiler_params=pltpu.CompilerParams(vmem_limit_bytes=48 * 2**20),
        cost_estimate=pl.CostEstimate(flops=2 * tokens * dl * ffl, bytes_accessed=2 * dl * ffl, transcendentals=0),
    )(og, gates, ups, gin)
    return grad_input, gwg, gwu, gwd


def solution(mesh):
    placed = (
        P("gy", "gx"),
        P("gx", "gy"),
        P("gx", "gy"),
        P("gy", "gx"),
        P("gx", "gy"),
        P("gx", "gy"),
        P("gy", "gx"),
    )
    return jax.shard_map(
        functools.partial(per_device, mesh.shape["gx"], mesh.shape["gy"]),
        mesh=mesh,
        in_specs=placed,
        out_specs=(P("gy", "gx"), P("gx", "gy"), P("gx", "gy"), P("gy", "gx")),
        check_vma=False,
    )
```

time: 302 us -> 163 us (0.54)
  waiting for transfers between devices: 171 us -> 0.02 us
  Pallas kernels: 0 us -> 138 us
  matrix products: 62.2 us -> 0 us
  local copies, waits for them, and re-layouts: 39.8 us -> 9.2 us
  blocking collectives: 11.2 us -> 0 us
    pallas_call x0 -> x3, Pallas kernels: none -> 138 us  [the longest x1 94.2 us: exchange(): pl.pallas_call(functools.partial(exchange_kernel, (A, B, G, K)), out_shap...]
    all_gather x3 -> x0, waiting for transfers between devices: 99.7 us -> none  [the longest x1 41.1 us: per_device(): gate_piece = lax.all_gather(d_gate, 'gx', axis=0, tiled=True)]
    reduce_scatter x2 -> x1, waiting for transfers between devices: 70.5 us -> 0.01 us  [per_device(): grad_input = lax.psum_scatter(gin, 'gy', scatter_dimension=0, tiled=True)]
    dot_general x6 -> x0, matrix products: 62.2 us -> none  [the longest x3 35.1 us: contract_cols(): lax.dot_general(left, right, (((1,), (1,)), ((), ())), preferred_element_...]
    unnamed x10 -> x14, local copies, waits for them, and re-layouts: 39.8 us -> 9.2 us
    all_gather x2 -> x0, blocking collectives: 11.2 us -> none  [the longest x1 6.24 us: per_device(): lax.all_gather(out_grad, 'gy', axis=0, tiled=True)]
  transfers between devices with their start and end apart: 5 -> 1, of which waited for: 4 -> 0; matrix products, arithmetic and copies ran while one was open for 30% -> 0% of each run, Pallas kernels for 0% -> 8%
where the time goes in v1:
time: 163 us; the launch traced here: 162 us
  Pallas kernels  138 us (85%)
  between operations  14.1 us (9%)
  local copies, waits for them, and re-layouts  9.2 us (6%)
    pallas_call x1, Pallas kernels, exchange(): pl.pallas_call(functools.partial(exchange_kernel, (A, B, G, K)), out_shap...  94.2 us
    pallas_call x1, Pallas kernels, per_device(): pl.pallas_call(gate_up_kernel, grid=(steps,), out_shape=(jax.ShapeDtypeSt...  30.5 us
    pallas_call x1, Pallas kernels, per_device(): pl.pallas_call(down_kernel, grid=(steps,), out_shape=jax.ShapeDtypeStruct...  13.7 us
    unnamed x14, local copies, waits for them, and re-layouts  9.2 us
  transfers between devices with their start and end apart: 1, of which 0 were waited for; matrix products, arithmetic and copies ran while one was open for 0% of the time, Pallas kernels for 8%

profile of v1, /device:TPU:0, one launch (start us, length us, event | category | flops | bytes accessed | tf_op | source)
XLA Modules:
  0.0 161.7 jit_solution(16246580924534338654)
XLA Ops:
  7.2 0.0 reduce-scatter.2.cloned.1.call-start
  7.2 0.0 copy-start.3
  7.2 0.9 copy-done.3
  8.2 0.0 copy-start.4
  8.2 0.9 copy-done.4
  9.1 0.0 copy-start.5
  9.1 0.8 copy-done.5
  9.9 0.0 copy-start.6
  9.9 0.8 copy-done.6
  10.8 94.2 %shard_map.102 = (bf16[7,16,8,2048]{3,2,1,0:T(8,128)(2,1)S(1)}, bf16[16,8,14336]{2,1,0:T(8,128)(2,1)S(1)}, bf16[16,8,14336]{2,1,0:T(8,128)(2,1)S(1)}, bf16[2,64,...) custom-call(bf16[64,512]{1,0:T(8,128)(2,1)S(1)} %copy-done.5, bf16[64,512]{1,0:T(8,128)(2,1)S(1)} %copy-done.6, ...), custom_call_target="tpu_custom_call" | custom-call | tf_op jit(solution)/shard_map/pallas_call | solution.py:294
  104.9 0.0 copy-start
  104.9 1.8 %copy-done = bf16[16,8,14336]{2,1,0:T(8,128)(2,1)} copy-done((bf16[16,8,14336]{2,1,0:T(8,128)(2,1)}, bf16[16,8,14336]{2,1,0:T(8,128)(2,1)S(1)}, u32[]{:S(2)}) %copy-start) | copy-done | bytes 3670040
  106.8 0.0 copy-start.2
  106.8 1.8 %copy-done.2 = bf16[16,8,14336]{2,1,0:T(8,128)(2,1)} copy-done((bf16[16,8,14336]{2,1,0:T(8,128)(2,1)}, bf16[16,8,14336]{2,1,0:T(8,128)(2,1)S(1)}, u32[]{:S(2)}) %copy-start.2) | copy-done | bytes 3670040
  108.6 30.5 %shard_map.103 = (bf16[128,512]{1,0:T(8,128)(2,1)}, bf16[512,14336]{1,0:T(8,128)(2,1)}, bf16[512,14336]{1,0:T(8,128)(2,1)}) custom-call(bf16[128,512]{1,0:T(8,128)(2,1)S(1)} %bitcast.3, bf16[7,16,8,2048]{3,2,1,0:T(8,128)(2,1)S(1)} %get-tuple-element.13.dh_ref, bf16[16,8,14336]{2,1,0:T(8,128)(2,1)} %copy-done, bf16[16,8,14336]{2,1,0:T(8,128)(2,1)} %copy-done.2, ...), custom_call_target="tpu_custom_call" | custom-call | flops 7516192768 | bytes 58720256 | tf_op jit(solution)/shard_map/pallas_call | solution.py:384
  139.1 0.0 reduce-scatter.2.cloned.1.call-update
  139.1 0.0 copy-start.1
  139.1 2.0 %copy-done.1 = bf16[16,8,14336]{2,1,0:T(8,128)(2,1)S(1)} copy-done((bf16[16,8,14336]{2,1,0:T(8,128)(2,1)S(1)}, bf16[16,8,14336]{2,1,0:T(8,128)(2,1)}, u32[]{:S(2)}) %copy-start.1) | copy-done | bytes 3670040
  141.2 13.7 %shard_map.104 = bf16[14336,512]{1,0:T(8,128)(2,1)} custom-call(bf16[128,512]{1,0:T(8,128)(2,1)S(1)} %bitcast.2, bf16[16,8,14336]{2,1,0:T(8,128)(2,1)S(1)} %copy-done.1, bf16[16,8,14336]{2,1,0:T(8,128)(2,1)} %copy-done.2, bf16[128,512]{1,0:T(8,128)(2,1)} %get-tuple-element.16.after_ref), custom_call_target="tpu_custom_call" | custom-call | flops 1879048192 | bytes 14680064 | tf_op jit(solution)/shard_map/pallas_call | solution.py:399
  154.9 0.0 reduce-scatter.2.cloned.1.call-done
Async XLA Ops:
  7.2 147.7 %reduce-scatter.2.cloned.1.call-start = ((), (), s32[]{:S(2)}) async-start(), calls=%async_computation.1 | async-start | bytes 196608 | tf_op jit(solution)/shard_map/reduce_scatter | solution.py:398
  7.2 0.9 copy-start.3
  8.2 0.9 copy-start.4
  9.1 0.8 copy-start.5
  9.9 0.8 copy-start.6
  104.9 1.8 %copy-start = (bf16[16,8,14336]{2,1,0:T(8,128)(2,1)}, bf16[16,8,14336]{2,1,0:T(8,128)(2,1)S(1)}, u32[]{:S(2)}) copy-start(bf16[16,8,14336]{2,1,0:T(8,128)(2,1)S(1)} %get-tuple-element.14.gate_ref) | copy-start | bytes 11010052
  106.8 1.8 %copy-start.2 = (bf16[16,8,14336]{2,1,0:T(8,128)(2,1)}, bf16[16,8,14336]{2,1,0:T(8,128)(2,1)S(1)}, u32[]{:S(2)}) copy-start(bf16[16,8,14336]{2,1,0:T(8,128)(2,1)S(1)} %get-tuple-element.15.up_ref) | copy-start | bytes 11010052
  139.1 2.0 %copy-start.1 = (bf16[16,8,14336]{2,1,0:T(8,128)(2,1)S(1)}, bf16[16,8,14336]{2,1,0:T(8,128)(2,1)}, u32[]{:S(2)}) copy-start(bf16[16,8,14336]{2,1,0:T(8,128)(2,1)} %copy-done) | copy-start | bytes 11010052
Sparse Core Ops, SparseCore 0:
  139.2 10.7 reduce-scatter.1

commit v2 on v1

--- a/solution.py
+++ b/solution.py
@@ -16,8 +16,10 @@
 
 def exchange_kernel(
     sizes,
-    x_ref, og_ref, gate_ref, up_ref, wd_ref,
-    dh_ref, gates_ref, ups_ref, xs_ref, ogs_ref,
+    x_ref, og_ref, gate_ref, up_ref, wd_ref, wg_ref, wu_ref,
+    gin_ref, dg_ref, du_ref, ht_ref, xs_ref, ogs_ref,
+    dh_ref, gates_ref, ups_ref, factor_gate, factor_up, g_buf, u_buf, h_out, g_out, u_out, acc,
+    gu_sem, h_sem, out_sem,
     w_buf, og_buf, part, core_in, sum_core, inner_in, sum_inner, outer_in, own,
     w_sem, local_sem, gy_send, gy_recv,
     rc_send, rc_recv, ri_send, ri_recv, ro_send, ro_recv,
@@ -73,12 +75,10 @@
     w_copy(0, 0).start()
     w_copy(1, 1).start()
 
-    def gy_copies(d):
+    def gy_copy(i, d):
         to = lax.rem(gy + d, G)
-        return (
-            remote(og_ref, og_buf.at[gy], gy_send.at[0, d - 1], gy_recv.at[0, d - 1], me, to),
-            remote(x_ref, xs_ref.at[gy], gy_send.at[1, d - 1], gy_recv.at[1, d - 1], me, to),
-        )
+        src, dst = ((og_ref, og_buf), (x_ref, xs_ref))[i]
+        return remote(src, dst.at[gy], gy_send.at[i, d - 1], gy_recv.at[i, d - 1], me, to)
 
     locals_ = [
         pltpu.make_async_copy(og_ref, og_buf.at[gy], local_sem.at[0]),
@@ -88,7 +88,7 @@
     ]
     locals_[0].start()
     for d in range(1, G):
-        gy_copies(d)[0].start()
+        gy_copy(0, d).start()
 
     def gather_ops(full, outer_s, outer_r, inner_s, inner_r, core_s, core_r):
         def to_outer(src, d):
@@ -131,7 +131,7 @@
                 to_inner(full(me), ai, e).wait_recv()
                 to_core(full(index(ai, bi, core)), ai, bi).start()
 
-    def finish(ops, full):
+    def finish_sends(ops, full):
         to_outer, to_inner, to_core = ops
         for d in range(1, A):
             to_outer(full(me), d).wait_send()
@@ -140,7 +140,13 @@
                 to_inner(full(me), ai, e).wait_send()
         for ai in range(A):
             for bi in range(B):
-                to_core(full(me), ai, bi).wait()
+                to_core(full(me), ai, bi).wait_send()
+
+    def finish_core(ops, full):
+        to_outer, to_inner, to_core = ops
+        for ai in range(A):
+            for bi in range(B):
+                to_core(full(me), ai, bi).wait_recv()
 
     saved = []
     for g, out in enumerate((gates_ref, ups_ref)):
@@ -159,12 +165,12 @@
     send_own(saved[0][0], gate_ref)
     send_own(saved[1][0], up_ref)
     for d in range(1, G):
-        gy_copies(d)[1].start()
+        gy_copy(1, d).start()
     for copy in locals_[1:]:
         copy.start()
     locals_[0].wait()
     for d in range(1, G):
-        gy_copies(d)[0].wait_recv()
+        gy_copy(0, d).wait_recv()
     og_out = pltpu.make_async_copy(og_buf, ogs_ref, local_sem.at[4])
     og_out.start()
 
@@ -248,21 +254,100 @@
 
     lax.fori_loop(0, K, add_outer, 0)
 
+    tokens = G * t
+    dl = og_ref.shape[1]
+
+    def columns(k):
+        return pl.ds(pl.multiple_of(k * cw, cw), cw)
+
+    def weight_copies(k, slot):
+        return (
+            pltpu.make_async_copy(wg_ref.at[:, columns(k)], g_buf.at[slot], gu_sem.at[0, slot]),
+            pltpu.make_async_copy(wu_ref.at[:, columns(k)], u_buf.at[slot], gu_sem.at[1, slot]),
+        )
+
+    def start_weights(k, slot):
+        for copy in weight_copies(k, slot):
+            copy.start()
+
+    def h_copy(k, slot):
+        return pltpu.make_async_copy(h_out.at[slot], ht_ref.at[columns(k)], h_sem.at[slot])
+
+    start_weights(0, 0)
+    start_weights(1, 1)
+    for copy in locals_[2:]:
+        copy.wait()
+    for ops, full in saved:
+        finish_core(ops, full)
+    acc[...] = jnp.zeros_like(acc)
+
+    def prepare(k):
+        slot = lax.rem(k, 2)
+        g = gates_ref[:, :, columns(k)].astype(F32).reshape(tokens, cw)
+        u = ups_ref[:, :, columns(k)].astype(F32).reshape(tokens, cw)
+        s = jax.nn.sigmoid(g)
+        silu = g * s
+        factor_up[k] = silu
+        factor_gate[k] = u * s * (1.0 + g * (1.0 - s))
+
+        @pl.when(k >= 2)
+        def _():
+            h_copy(k - 2, slot).wait()
+        h_out[slot] = (silu * u).T.astype(BF16)
+        h_copy(k, slot).start()
+
     def forward_outer(k, _):
         pass_outer(*hidden_ops(k))
+        prepare(k)
         return 0
 
     lax.fori_loop(0, K, forward_outer, 0)
 
+    def out_copies(k, slot):
+        return (
+            pltpu.make_async_copy(g_out.at[slot], dg_ref.at[:, columns(k)], out_sem.at[0, slot]),
+            pltpu.make_async_copy(u_out.at[slot], du_ref.at[:, columns(k)], out_sem.at[1, slot]),
+        )
+
+    def process(k):
+        slot = lax.rem(k, 2)
+        finish_core(*hidden_ops(k))
+        own_copy(k).wait()
+        dh = dh_ref[k].astype(F32).reshape(tokens, cw)
+
+        @pl.when(k >= 2)
+        def _():
+            for copy in out_copies(k - 2, slot):
+                copy.wait()
+        g_out[slot] = (dh * factor_gate[k]).astype(BF16)
+        u_out[slot] = (dh * factor_up[k]).astype(BF16)
+        for copy in out_copies(k, slot):
+            copy.start()
+        for copy in weight_copies(k, slot):
+            copy.wait()
+        dims = (((1,), (1,)), ((), ()))
+        acc[...] += lax.dot_general(g_out[slot], g_buf[slot], dims, preferred_element_type=F32)
+        acc[...] += lax.dot_general(u_out[slot], u_buf[slot], dims, preferred_element_type=F32)
+
+        @pl.when(k + 2 < K)
+        def _():
+            start_weights(k + 2, slot)
+
     def forward_inner(k, _):
-        pass_inner(*hidden_ops(k))
-        return 0
-
-    lax.fori_loop(0, K, forward_inner, 0)
+        @pl.when(k < K)
+        def _():
+            pass_inner(*hidden_ops(k))
+
+        @pl.when(k >= 1)
+        def _():
+            process(k - 1)
+        return 0
+
+    lax.fori_loop(0, K + 1, forward_inner, 0)
+    gin_ref[...] = acc[...].astype(BF16)
 
     def close(k, _):
-        finish(*hidden_ops(k))
-        own_copy(k).wait()
+        finish_sends(*hidden_ops(k))
         core_copy(k).wait_send()
         for e in range(1, B):
             inner_copy(k, e).wait_send()
@@ -271,18 +356,20 @@
         return 0
 
     lax.fori_loop(0, K, close, 0)
+    for k in (K - 2, K - 1):
+        h_copy(k, k % 2).wait()
+        for copy in out_copies(k, k % 2):
+            copy.wait()
     for ops, full in saved:
-        finish(ops, full)
-    for copy in locals_[1:]:
-        copy.wait()
+        finish_sends(ops, full)
+    locals_[1].wait()
     og_out.wait()
     for d in range(1, G):
-        og_copy, x_copy = gy_copies(d)
-        og_copy.wait_send()
-        x_copy.wait()
-
-
-def exchange(n, G, x, og, gate, up, wd):
+        gy_copy(0, d).wait_send()
+        gy_copy(1, d).wait()
+
+
+def exchange(n, G, x, og, gate, up, wd, wg, wu):
     A = OUTER if n % (2 * OUTER) == 0 else 1
     B = n // (2 * A)
     K = CHUNKS
@@ -294,15 +381,28 @@
     return pl.pallas_call(
         functools.partial(exchange_kernel, (A, B, G, K)),
         out_shape=(
-            jax.ShapeDtypeStruct((K, n, rows, cw), BF16),
-            jax.ShapeDtypeStruct((n, rows, ffl), BF16),
-            jax.ShapeDtypeStruct((n, rows, ffl), BF16),
+            jax.ShapeDtypeStruct((G * t, dl), BF16),
+            jax.ShapeDtypeStruct((G * t, ffl), BF16),
+            jax.ShapeDtypeStruct((G * t, ffl), BF16),
+            jax.ShapeDtypeStruct((ffl, G * t), BF16),
             jax.ShapeDtypeStruct((G, t, dl), BF16),
             jax.ShapeDtypeStruct((G, t, dl), BF16),
         ),
-        in_specs=[any_spec] * 5,
-        out_specs=(any_spec,) * 5,
+        in_specs=[any_spec] * 7,
+        out_specs=(pl.BlockSpec(memory_space=pltpu.VMEM),) + (any_spec,) * 5,
         scratch_shapes=[
+            pltpu.VMEM((K, n, rows, cw), BF16),
+            pltpu.VMEM((n, rows, ffl), BF16),
+            pltpu.VMEM((n, rows, ffl), BF16),
+            pltpu.VMEM((K, G * t, cw), F32),
+            pltpu.VMEM((K, G * t, cw), F32),
+            pltpu.VMEM((2, dl, cw), BF16),
+            pltpu.VMEM((2, dl, cw), BF16),
+            pltpu.VMEM((2, cw, G * t), BF16),
+            pltpu.VMEM((2, G * t, cw), BF16),
+            pltpu.VMEM((2, G * t, cw), BF16),
+            pltpu.VMEM((G * t, dl), F32),
+            dma((2, 2)), dma((2,)), dma((2, 2)),
             pltpu.VMEM((2, cw, dl), BF16),
             pltpu.VMEM((G, t, dl), BF16),
             pltpu.VMEM((K, A, B, 2, rows, cw), BF16),
@@ -324,87 +424,47 @@
             dma((K,)),
         ],
         compiler_params=pltpu.CompilerParams(
-            collective_id=0, has_side_effects=True, vmem_limit_bytes=32 * 2**20
+            collective_id=0, has_side_effects=True, vmem_limit_bytes=62 * 2**20
         ),
-    )(x, og, gate, up, wd)
-
-
-def gate_up_kernel(x_ref, dh_ref, gate_ref, up_ref, wg_ref, wu_ref, gin_ref, gwg_ref, gwu_ref, xt, acc):
-    step = pl.program_id(0)
-    tokens, dl = x_ref.shape
-
-    @pl.when(step == 0)
+    )(x, og, gate, up, wd, wg, wu)
+
+
+def weights_kernel(x_ref, og_ref, dg_ref, du_ref, ht_ref, gwg_ref, gwu_ref, gwd_ref, xt):
+    @pl.when(pl.program_id(0) == 0)
     def _():
         xt[...] = x_ref[...].astype(F32).T.astype(BF16)
-        acc[...] = jnp.zeros_like(acc)
-
-    width = gate_ref.shape[2]
-    g = gate_ref[...].astype(F32).reshape(tokens, width)
-    u = up_ref[...].astype(F32).reshape(tokens, width)
-    dh = dh_ref[0].astype(F32).reshape(tokens, width)
-    s = jax.nn.sigmoid(g)
-    d_up = (dh * (g * s)).astype(BF16)
-    d_gate = (dh * u * s * (1.0 + g * (1.0 - s))).astype(BF16)
-    gwg_ref[...] = jnp.dot(xt[...], d_gate, preferred_element_type=F32).astype(BF16)
-    gwu_ref[...] = jnp.dot(xt[...], d_up, preferred_element_type=F32).astype(BF16)
-    dims = (((1,), (1,)), ((), ()))
-    acc[...] += lax.dot_general(d_gate, wg_ref[...], dims, preferred_element_type=F32) + lax.dot_general(
-        d_up, wu_ref[...], dims, preferred_element_type=F32
-    )
-
-    @pl.when(step == pl.num_programs(0) - 1)
-    def _():
-        gin_ref[...] = acc[...].astype(BF16)
-
-
-def down_kernel(og_ref, gate_ref, up_ref, after_ref, gwd_ref):
-    tokens, dl = og_ref.shape
-    width = gate_ref.shape[2]
-    g = gate_ref[...].astype(F32).reshape(tokens, width)
-    u = up_ref[...].astype(F32).reshape(tokens, width)
-    hidden = (g * jax.nn.sigmoid(g) * u).astype(BF16)
-    gwd_ref[...] = lax.dot_general(
-        hidden, og_ref[...], (((0,), (0,)), ((), ())), preferred_element_type=F32
-    ).astype(BF16)
+
+    gwg_ref[...] = jnp.dot(xt[...], dg_ref[...], preferred_element_type=F32).astype(BF16)
+    gwu_ref[...] = jnp.dot(xt[...], du_ref[...], preferred_element_type=F32).astype(BF16)
+    gwd_ref[...] = jnp.dot(ht_ref[...], og_ref[...], preferred_element_type=F32).astype(BF16)
 
 
 def per_device(n, G, inputs, gate_pre, up_pre, out_grad, w_gate, w_up, w_down):
-    dh, gates, ups, xs, ogs = exchange(n, G, inputs, out_grad, gate_pre, up_pre, w_down)
-    K, _, rows, cw = dh.shape
+    gin, dg, du, ht, xs, ogs = exchange(n, G, inputs, out_grad, gate_pre, up_pre, w_down, w_gate, w_up)
     dl, ffl = w_gate.shape
-    tokens = n * rows
-    x = xs.reshape(tokens, dl)
-    og = ogs.reshape(tokens, dl)
-    width = 1024 if cw % 1024 == 0 else cw
-    per = cw // width
-    steps = ffl // width
+    tokens = dg.shape[0]
+    grad_input = lax.psum_scatter(gin, "gy", scatter_dimension=0, tiled=True)
+    width = 1024 if ffl % 1024 == 0 else 512
     whole = pl.BlockSpec((tokens, dl), lambda k: (0, 0))
-    act = pl.BlockSpec((n, rows, width), lambda k: (0, 0, k))
+    act = pl.BlockSpec((tokens, width), lambda k: (0, k))
     wide = pl.BlockSpec((dl, width), lambda k: (0, k))
-    gin, gwg, gwu = pl.pallas_call(
-        gate_up_kernel,
-        grid=(steps,),
+    gwg, gwu, gwd = pl.pallas_call(
+        weights_kernel,
+        grid=(ffl // width,),
         out_shape=(
-            jax.ShapeDtypeStruct((tokens, dl), BF16),
             jax.ShapeDtypeStruct((dl, ffl), BF16),
             jax.ShapeDtypeStruct((dl, ffl), BF16),
+            jax.ShapeDtypeStruct((ffl, dl), BF16),
         ),
-        in_specs=[whole, pl.BlockSpec((1, n, rows, width), lambda k: (k // per, 0, 0, k % per)), act, act, wide, wide],
-        out_specs=(whole, wide, wide),
-        scratch_shapes=[pltpu.VMEM((dl, tokens), BF16), pltpu.VMEM((tokens, dl), F32)],
-        compiler_params=pltpu.CompilerParams(vmem_limit_bytes=48 * 2**20),
-        cost_estimate=pl.CostEstimate(flops=8 * tokens * dl * ffl, bytes_accessed=8 * dl * ffl, transcendentals=0),
-    )(x, dh, gates, ups, w_gate, w_up)
-    grad_input = lax.psum_scatter(gin, "gy", scatter_dimension=0, tiled=True)
-    gwd = pl.pallas_call(
-        down_kernel,
-        grid=(steps,),
-        out_shape=jax.ShapeDtypeStruct((ffl, dl), BF16),
-        in_specs=[whole, act, act, pl.BlockSpec(memory_space=pl.ANY)],
-        out_specs=pl.BlockSpec((width, dl), lambda k: (k, 0)),
-        compiler_params=pltpu.CompilerParams(vmem_limit_bytes=48 * 2**20),
-        cost_estimate=pl.CostEstimate(flops=2 * tokens * dl * ffl, bytes_accessed=2 * dl * ffl, transcendentals=0),
-    )(og, gates, ups, gin)
+        in_specs=[
+            whole, whole, act, act,
+            pl.BlockSpec((width, tokens), lambda k: (k, 0)),
+        ],
+        out_specs=(wide, wide, pl.BlockSpec((width, dl), lambda k: (k, 0))),
+        scratch_shapes=[pltpu.VMEM((dl, tokens), BF16)],
+        compiler_params=pltpu.CompilerParams(vmem_limit_bytes=62 * 2**20),
+        cost_estimate=pl.CostEstimate(flops=6 * tokens * dl * ffl, bytes_accessed=8 * dl * ffl, transcendentals=0),
+    )(xs.reshape(tokens, dl), ogs.reshape(tokens, dl), dg, du, ht)
     return grad_input, gwg, gwu, gwd
 
 

time: 163 us -> 142 us (0.87)
  Pallas kernels: 138 us -> 126 us
  local copies, waits for them, and re-layouts: 9.2 us -> 0 us
    pallas_call x2 -> x1, Pallas kernels: 44.2 us -> 20.7 us  [per_device(): pl.pallas_call(weights_kernel, grid=(ffl // width,), out_shape=(jax.Shape...]
    pallas_call x1, Pallas kernels: 94.2 us -> 106 us  [exchange(): pl.pallas_call(functools.partial(exchange_kernel, (A, B, G, K)), out_shap...]
    unnamed x14 -> x0, local copies, waits for them, and re-layouts: 9.2 us -> none
  transfers between devices with their start and end apart: 1 -> 1, of which waited for: 0 -> 0; matrix products, arithmetic and copies ran while one was open for 0% -> 0% of each run, Pallas kernels for 8% -> 15%
where the time goes in v2:
time: 142 us; the launch traced here: 140 us
  Pallas kernels  126 us (89%)
  between operations  14 us (10%)
    pallas_call x1, Pallas kernels, exchange(): pl.pallas_call(functools.partial(exchange_kernel, (A, B, G, K)), out_shap...  106 us
    pallas_call x1, Pallas kernels, per_device(): pl.pallas_call(weights_kernel, grid=(ffl // width,), out_shape=(jax.Shape...  20.7 us
  transfers between devices with their start and end apart: 1, of which 0 were waited for; matrix products, arithmetic and copies ran while one was open for 0% of the time, Pallas kernels for 15%

profile of v2, /device:TPU:0, one launch (start us, length us, event | category | flops | bytes accessed | tf_op | source)
XLA Modules:
  0.0 140.3 jit_solution(14193429273071092177)
XLA Ops:
  7.2 0.0 reduce-scatter.2.cloned.1.call-start
  7.2 105.5 %shard_map.102 = (bf16[128,512]{1,0:T(8,128)(2,1)}, bf16[128,14336]{1,0:T(8,128)(2,1)}, bf16[128,14336]{1,0:T(8,128)(2,1)}, bf16[14336,128]{1,0:T(8,128)(2,1)}, ...) custom-call(bf16[64,512]{1,0:T(8,128)(2,1)} %x_ref.1, bf16[64,512]{1,0:T(8,128)(2,1)} %og_ref.1, ...), custom_call_target="tpu_custom_call" | custom-call | tf_op jit(solution)/shard_map/pallas_call | solution.py:381
  112.8 0.0 reduce-scatter.2.cloned.1.call-update
  112.8 20.7 %shard_map.103 = (bf16[512,14336]{1,0:T(8,128)(2,1)}, bf16[512,14336]{1,0:T(8,128)(2,1)}, bf16[14336,512]{1,0:T(8,128)(2,1)}) custom-call(bf16[128,512]{1,0:T(8,128)(2,1)} %bitcast.2, bf16[128,512]{1,0:T(8,128)(2,1)} %bitcast.3, bf16[128,14336]{1,0:T(8,128)(2,1)} %get-tuple-element.16.dg_ref, bf16[128,14336]{1,0:T(8,128)(2,1)} %get-tuple-element.17.du_ref, ...), custom_call_target="tpu_custom_call" | custom-call | flops 5637144576 | bytes 58720256 | tf_op jit(solution)/shard_map/pallas_call | solution.py:451
  133.5 0.0 reduce-scatter.2.cloned.1.call-done
Async XLA Ops:
  7.2 126.3 %reduce-scatter.2.cloned.1.call-start = ((), (), s32[]{:S(2)}) async-start(), calls=%async_computation.1 | async-start | bytes 196608 | tf_op jit(solution)/shard_map/reduce_scatter | solution.py:446
Sparse Core Ops, SparseCore 0:
  112.9 9.9 reduce-scatter.1
